TPU v7x, 512 devices: a whole 4x4x16 slice. The times are simulated.
512 devices in a mesh: ctx: 32 (over x_hi, z), fsdp: 16 (over y, x_lo, core).
Axes of the slice: x: 4 (x_hi: 2, x_lo: 2; x = x_hi * 2 + x_lo), y: 4, z: 16, core: 2. Of those that a mesh axis runs over, the one named last changes fastest.
Arguments:
- streams: bfloat16 [3, 16384, 8192], P(None, ('ctx', 'fsdp')), may hold values from -6 to 6
- segments: int32 [16384], replicated, may hold values from 0 to 63, never falling along the last dimension, each value on 1 to 4096 neighbouring positions
- short_taps: float32 [3, 3, 8192], P(None, None, 'fsdp'), may hold values from -3 to 3
- decay_rates: float32 [512, 16], P('fsdp'), may hold values from 1.2207031e-05 to 0.1
- residues: float32 [512, 16], P('fsdp'), may hold values from -2 to 2
- skip_gain: float32 [8192], P('fsdp'), may hold values from -4 to 4
Outputs:
- output: bfloat16 [16384, 8192], P(('ctx', 'fsdp'))
Inputs may be any that keep to these rules, and one draw needn't show every extreme that they name: `segments`: never falling along the window; every document has 1 to 4096 tokens and one has exactly 4096.
All inputs are finite; a program needn't handle non-finite values.
Results may differ from a plain program's by a relative error of at most 0.0064.
Values may be sent and summed in bfloat16 or wider, within the bound.
A program may use at most 64 MiB of HBM per device.

v0:
```python
import jax
import jax.numpy as jnp
from jax import lax
from jax.sharding import PartitionSpec as P

GROUP = 16
MODES = 16
SHORT = 3
SPAN = 8


def shifted_2(block, axis, distance):
    devices = range(lax.axis_size(axis))
    route = [(i - distance, i) for i in devices if i - distance in devices]
    return lax.ppermute(block, axis, route)


def contract(pattern, left_side, right_side):
    return jnp.einsum(pattern, left_side, right_side, precision=lax.Precision.HIGHEST)


def featurize(block_rows, before_rows, tap_rows, row_marks, before_marks):
    margin = before_rows.shape[1]
    row_count = block_rows.shape[1]
    joined = jnp.concatenate([before_rows, block_rows], axis=1)
    all_marks = jnp.concatenate([before_marks, row_marks])
    summed = block_rows.astype(jnp.float32) * tap_rows[:, 0][:, None, :]
    for offset in range(1, margin + 1):
        shifted = joined[:, margin - offset : margin - offset + row_count].astype(jnp.float32)
        agreeing = all_marks[margin - offset : margin - offset + row_count] == row_marks
        summed = (
            summed
            + jnp.where(agreeing[None, :, None], shifted, 0.0) * tap_rows[:, offset][:, None, :]
        )
    queries = summed[0].astype(jnp.bfloat16)
    gated_prod = (summed[1] * summed[2]).astype(jnp.bfloat16)
    return lax.optimization_barrier((queries, gated_prod))


def tile_filter(gated_prod, tile_marks, decay_rates, mode_gain, rising):
    tile_rows, channels = gated_prod.shape
    groups = channels // GROUP
    block_len = min(128, tile_rows)
    offsets = jnp.arange(block_len, dtype=jnp.float32)
    forward = mode_gain[:, :, None] * jnp.exp(-decay_rates[:, :, None] * offsets)
    backward = jnp.exp(decay_rates[:, :, None] * offsets)
    causal = (offsets[:, None] >= offsets[None, :]).astype(jnp.float32)
    kernel = contract("gmt,gms->gts", forward, backward) * causal
    mode_rates = decay_rates.T[:, :, None]
    closing = jnp.exp(-mode_rates * (block_len - 1.0 - offsets))
    through = jnp.exp(-mode_rates * block_len)
    head_rising = rising[:, :, :block_len]
    values = gated_prod.astype(jnp.float32).reshape(tile_rows, groups, GROUP)
    carried = jnp.zeros((MODES, groups, GROUP), jnp.float32)
    last_seen = jnp.int32(-1)
    pieces = []
    for number in range(tile_rows // block_len):
        block_vals = values[number * block_len : (number + 1) * block_len]
        block_marks = tile_marks[number * block_len : (number + 1) * block_len]
        agreeing = (block_marks[:, None] == block_marks[None, :]).astype(jnp.float32)
        inside = contract("gts,sgc->tgc", kernel * agreeing, block_vals)
        follow = (block_marks == last_seen).astype(jnp.float32)
        inside = inside + follow[:, None, None] * contract("mgt,mgc->tgc", head_rising, carried)
        ending = (block_marks == block_marks[block_len - 1]).astype(jnp.float32)
        fresh_state = contract("mgs,sgc->mgc", closing * ending, block_vals)
        passing = (block_marks[block_len - 1] == last_seen).astype(jnp.float32)
        carried = fresh_state + passing * through * carried
        last_seen = block_marks[block_len - 1]
        pieces.append(inside)
    return (jnp.concatenate(pieces, axis=0), carried)


def local(streams, segments, short_taps, decay_rates, residues, skip_gain):
    fsdp_count = lax.axis_size("fsdp")
    ctx_count = lax.axis_size("ctx")
    tile_index = lax.axis_index("ctx")
    own_rows = streams.shape[1]
    tile_rows = own_rows * fsdp_count
    margin = SHORT - 1
    padded_marks = jnp.concatenate([jnp.full((margin,), -1, jnp.int32), segments])
    tile_start = tile_index * tile_rows
    tile_marks = lax.dynamic_slice_in_dim(segments, tile_start, tile_rows)
    local_streams = lax.all_to_all(streams, "fsdp", split_axis=2, concat_axis=1, tiled=True)
    before_rows = shifted_2(local_streams[:, tile_rows - margin :, :], "ctx", 1)
    before_marks = lax.dynamic_slice_in_dim(padded_marks, tile_start, margin)
    queries, gated_prod = featurize(
        local_streams, before_rows, short_taps, tile_marks, before_marks
    )
    channels = gated_prod.shape[1]
    groups = channels // GROUP
    mode_gain = residues * jnp.sqrt(-jnp.expm1(-2.0 * decay_rates))
    positions = jnp.arange(tile_rows, dtype=jnp.float32)
    mode_rates = decay_rates.T[:, :, None]
    rising = mode_gain.T[:, :, None] * jnp.exp(-mode_rates * (positions + 1.0))
    local_part, end_state = tile_filter(gated_prod, tile_marks, decay_rates, mode_gain, rising)
    first_mark = tile_marks[0]
    falling = jnp.exp(-mode_rates * (tile_rows - 1.0 - positions))

    def source_state(operand):
        source_vals, source_marks = operand
        chosen = (source_marks == first_mark).astype(jnp.float32)
        return contract(
            "mgs,sgc->mgc",
            falling * chosen,
            source_vals.astype(jnp.float32).reshape(tile_rows, groups, GROUP),
        )

    def empty_state(operand):
        return jnp.zeros((MODES, groups, GROUP), jnp.float32)

    prior_state = jnp.zeros((MODES, groups, GROUP), jnp.float32)
    for distance in range(1, min(SPAN, ctx_count - 1) + 1):
        source_tile = shifted_2(gated_prod, "ctx", distance)
        source_index = tile_index - distance
        source_marks = lax.dynamic_slice_in_dim(
            segments, jnp.maximum(source_index, 0) * tile_rows, tile_rows
        )
        paired = (source_index >= 0) & (source_marks[tile_rows - 1] == first_mark)
        received = lax.cond(paired, source_state, empty_state, (source_tile, source_marks))
        prior_state = prior_state + jnp.exp(-mode_rates * ((distance - 1) * tile_rows)) * received
    prior_mark = first_mark.astype(jnp.float32)
    follow_tile = (tile_marks.astype(jnp.float32) == prior_mark).astype(jnp.float32)
    filtered = local_part + follow_tile[:, None, None] * contract(
        "mgt,mgc->tgc", rising, prior_state
    )
    mixed_out = (
        filtered.reshape(tile_rows, channels) + skip_gain * gated_prod.astype(jnp.float32)
    ).astype(jnp.bfloat16)
    mixed_out = lax.optimization_barrier(mixed_out)
    payload = (queries.astype(jnp.float32) * mixed_out.astype(jnp.float32)).astype(jnp.bfloat16)
    returned = lax.all_to_all(payload, "fsdp", split_axis=0, concat_axis=1, tiled=True)
    return returned


def solution(mesh):
    placed = (
        P(None, ("ctx", "fsdp"), None),
        P(),
        P(None, None, "fsdp"),
        P("fsdp", None),
        P("fsdp", None),
        P("fsdp"),
    )
    return jax.shard_map(
        local, mesh=mesh, in_specs=placed, out_specs=P(("ctx", "fsdp"), None), check_vma=False
    )
```

profile of v0, /device:TPU:4, one launch (start us, length us, event | category | flops | bytes accessed | tf_op | source)
XLA Modules:
  0.0 510.9 jit_solution(597949325799028393)
XLA Ops:
  0.0 10.6 %copy.91 = bf16[3,32,8192]{1,0,2:T(4,128)(2,1)} copy(bf16[3,32,8192]{2,1,0:T(8,128)(2,1)} %param.22) | data formatting | bytes 3145728 | tf_op args[0]
  10.6 13.2 %reshape.234 = bf16[16,2,24576]{2,1,0:T(2,128)(2,1)} reshape(bf16[8192,3,32]{2,1,0:T(4,128)(2,1)} %bitcast.120) | data formatting | bytes 3145728
  23.8 5.4 %all-to-all-start = ((bf16[16,2,24576]{2,1,0:T(2,128)(2,1)}), bf16[16,2,24576]{2,1,0:T(2,128)(2,1)}, u32[]{:S(2)}, u32[]{:S(2)}) async-start(bf16[16,2,24576]{2,1,0:T(2,128)(2,1)} %reshape.234), calls=%async_computation | async-start | bytes 3145728 | tf_op jit(solution)/shard_map/all_to_all | solution.py:83
  33.3 2.5 compare_convert_fusion.18
  41.6 3.7 fusion.87
  45.3 6.2 %all-to-all-done = bf16[16,2,24576]{2,1,0:T(2,128)(2,1)} async-done(((bf16[16,2,24576]{2,1,0:T(2,128)(2,1)}), bf16[16,2,24576]{2,1,0:T(2,128)(2,1)}, u32[]{:S(2)}, u32[]{:S(2)}) %all-to-all-start) | async-done | bytes 1572896 | tf_op jit(solution)/shard_map/all_to_all | solution.py:83
  51.5 12.6 %reshape.235 = bf16[8192,3,32]{2,1,0:T(4,128)(2,1)} reshape(bf16[16,2,24576]{2,1,0:T(2,128)(2,1)} %all-to-all-done) | data formatting | bytes 3145728
  64.1 11.8 %copy.128 = bf16[3,32,16,512]{3,1,2,0:T(8,128)(2,1)} copy(bf16[3,32,16,512]{1,0,3,2:T(4,128)(2,1)} %bitcast.119) | data formatting | bytes 3145728 | tf_op jit(solution)/shard_map/all_to_all | solution.py:83
  76.6 3.8 collective-permute-start
  103.3 3.9 multiply_add_fusion
  109.0 1.8 fusion.125
  110.8 14.8 %collective-permute-start.8 = (bf16[512,512]{1,0:T(8,128)(2,1)}, bf16[512,512]{1,0:T(8,128)(2,1)}, u32[]{:S(2)}, u32[]{:S(2)}) collective-permute-start(bf16[512,512]{1,0:T(8,128)(2,1)} %fusion.68), channel_id=1, source_target_pairs={{0,128},{16,144},{32,160},{48,176},{64,192},{80,208},{96,224},{112... | collective-permute-start | bytes 1572872 | tf_op jit(solution)/shard_map/ppermute | solution.py:15
  125.7 4.0 collective-permute-start.7
  129.7 3.1 collective-permute-start.6
  132.8 1.9 collective-permute-start.5
  134.7 2.1 collective-permute-start.4
  138.0 1.7 copy.94
  139.7 1.7 copy.105
  141.3 1.4 fusion.57
  142.8 1.3 convolution_multiply_fusion.3
  146.3 2.5 fusion.40
  148.8 2.5 fusion.46
  151.7 2.5 fusion.34
  154.2 13.2 %collective-permute-start.3 = (bf16[512,512]{1,0:T(8,128)(2,1)}, bf16[512,512]{1,0:T(8,128)(2,1)}, u32[]{:S(2)}, u32[]{:S(2)}) collective-permute-start(bf16[512,512]{1,0:T(8,128)(2,1)} %fusion.68), channel_id=1, source_target_pairs={{0,48},{16,64},{32,80},{48,96},{64,112},{80,128},{96,144},{112,160... | collective-permute-start | bytes 1572872 | tf_op jit(solution)/shard_map/ppermute | solution.py:15
  167.4 104.7 %collective-permute-done.7 = bf16[512,512]{1,0:T(8,128)(2,1)} collective-permute-done((bf16[512,512]{1,0:T(8,128)(2,1)}, bf16[512,512]{1,0:T(8,128)(2,1)}, u32[]{:S(2)}, u32[]{:S(2)}) %collective-permute-start.7) | collective-permute-done | bytes 524320 | tf_op jit(solution)/shard_map/ppermute | solution.py:15
  272.0 17.1 %collective-permute-start.2 = (bf16[512,512]{1,0:T(8,128)(2,1)}, bf16[512,512]{1,0:T(8,128)(2,1)}, u32[]{:S(2)}, u32[]{:S(2)}) collective-permute-start(bf16[512,512]{1,0:T(8,128)(2,1)} %fusion.68), channel_id=1, source_target_pairs={{0,32},{16,48},{32,64},{48,80},{64,96},{80,112},{96,128},{112,144}... | collective-permute-start | bytes 1572872 | tf_op jit(solution)/shard_map/ppermute | solution.py:15
  289.2 59.7 %collective-permute-done.6 = bf16[512,512]{1,0:T(8,128)(2,1)} collective-permute-done((bf16[512,512]{1,0:T(8,128)(2,1)}, bf16[512,512]{1,0:T(8,128)(2,1)}, u32[]{:S(2)}, u32[]{:S(2)}) %collective-permute-start.6) | collective-permute-done | bytes 524320 | tf_op jit(solution)/shard_map/ppermute | solution.py:15
  348.9 1.9 collective-permute-start.1
  351.2 2.5 fusion.52
  354.3 2.6 conditional.14
  357.0 2.6 conditional.13
  357.0 1.3 copy.118
  359.6 2.7 conditional.12
  359.7 1.3 copy.116
  362.3 73.8 %collective-permute-done.4 = bf16[512,512]{1,0:T(8,128)(2,1)} collective-permute-done((bf16[512,512]{1,0:T(8,128)(2,1)}, bf16[512,512]{1,0:T(8,128)(2,1)}, u32[]{:S(2)}, u32[]{:S(2)}) %collective-permute-start.4) | collective-permute-done | bytes 524320 | tf_op jit(solution)/shard_map/ppermute | solution.py:15
  436.2 2.6 conditional.11
  436.2 1.3 copy.114
  438.8 14.5 %collective-permute-done.3 = bf16[512,512]{1,0:T(8,128)(2,1)} collective-permute-done((bf16[512,512]{1,0:T(8,128)(2,1)}, bf16[512,512]{1,0:T(8,128)(2,1)}, u32[]{:S(2)}, u32[]{:S(2)}) %collective-permute-start.3) | collective-permute-done | bytes 524320 | tf_op jit(solution)/shard_map/ppermute | solution.py:15
  453.4 2.6 conditional.10
  453.4 1.3 copy.112
  455.9 18.9 %collective-permute-done.2 = bf16[512,512]{1,0:T(8,128)(2,1)} collective-permute-done((bf16[512,512]{1,0:T(8,128)(2,1)}, bf16[512,512]{1,0:T(8,128)(2,1)}, u32[]{:S(2)}, u32[]{:S(2)}) %collective-permute-start.2) | collective-permute-done | bytes 524320 | tf_op jit(solution)/shard_map/ppermute | solution.py:15
  474.8 2.6 conditional.9
  477.5 8.3 %collective-permute-done.1 = bf16[512,512]{1,0:T(8,128)(2,1)} collective-permute-done((bf16[512,512]{1,0:T(8,128)(2,1)}, bf16[512,512]{1,0:T(8,128)(2,1)}, u32[]{:S(2)}, u32[]{:S(2)}) %collective-permute-start.1) | collective-permute-done | bytes 524320 | tf_op jit(solution)/shard_map/ppermute | solution.py:15
  485.9 4.0 conditional.8
  487.1 1.3 compare_convert_fusion
  488.4 1.5 convolution_bitcast_fusion
  490.0 3.3 fusion.30
  495.3 14.7 %all_to_all.37 = bf16[16,32,512]{2,1,0:T(8,128)(2,1)S(1)} all-to-all(bf16[16,32,512]{2,1,0:T(8,128)(2,1)S(1)} %bitcast.124), channel_id=1, replica_groups=mesh['ctx'=32,'fsdp'=16] {'fsdp'}, dimensions={0} | all-to-all | bytes 1048576 | tf_op jit(solution)/shard_map/all_to_all | solution.py:131
  (164 shorter events, 40.8 us)
Async XLA Ops:
  23.8 5.5 %copy-start.11 = (s32[16384]{0:T(1024)S(1)}, s32[16384]{0:T(1024)}, u32[]{:S(2)}) copy-start(s32[16384]{0:T(1024)} %param.23) | copy-start | bytes 196612
  23.8 12.0 %copy-start.22 = (f32[3,3,512]{2,1,0:T(4,128)S(1)}, f32[3,3,512]{2,1,0:T(4,128)}, u32[]{:S(2)}) copy-start(f32[3,3,512]{2,1,0:T(4,128)} %param.24) | copy-start | bytes 55300
  23.8 13.5 %copy-start.12 = (f32[32,16]{0,1:T(8,128)S(1)}, f32[32,16]{0,1:T(8,128)}, u32[]{:S(2)}) copy-start(f32[32,16]{0,1:T(8,128)} %param.25) | copy-start | bytes 6148
  23.8 13.5 %copy-start.23 = (f32[32,16]{0,1:T(8,128)S(1)}, f32[32,16]{0,1:T(8,128)}, u32[]{:S(2)}) copy-start(f32[32,16]{0,1:T(8,128)} %param.26) | copy-start | bytes 6148
  23.8 27.7 %all-to-all-start = ((bf16[16,2,24576]{2,1,0:T(2,128)(2,1)}), bf16[16,2,24576]{2,1,0:T(2,128)(2,1)}, u32[]{:S(2)}, u32[]{:S(2)}) async-start(bf16[16,2,24576]{2,1,0:T(2,128)(2,1)} %reshape.234), calls=%async_computation | async-start | bytes 3145728 | tf_op jit(solution)/shard_map/all_to_all | solution.py:83
  29.4 53.6 %copy-start.37 = (s32[512]{0:T(512)}, s32[512]{0:T(512)S(1)}, u32[]{:S(2)}) copy-start(s32[512]{0:T(512)S(1)} %get-tuple-element.236) | copy-start | bytes 6148
  29.4 55.5 %copy-start.35 = (s32[512]{0:T(512)}, s32[512]{0:T(512)S(1)}, u32[]{:S(2)}) copy-start(s32[512]{0:T(512)S(1)} %get-tuple-element.237) | copy-start | bytes 6148
  29.4 57.3 %copy-start.33 = (s32[512]{0:T(512)}, s32[512]{0:T(512)S(1)}, u32[]{:S(2)}) copy-start(s32[512]{0:T(512)S(1)} %get-tuple-element.230) | copy-start | bytes 6148
  29.4 59.2 %copy-start.31 = (s32[512]{0:T(512)}, s32[512]{0:T(512)S(1)}, u32[]{:S(2)}) copy-start(s32[512]{0:T(512)S(1)} %get-tuple-element.231) | copy-start | bytes 6148
  29.4 61.0 %copy-start.29 = (s32[512]{0:T(512)}, s32[512]{0:T(512)S(1)}, u32[]{:S(2)}) copy-start(s32[512]{0:T(512)S(1)} %get-tuple-element.232) | copy-start | bytes 6148
  29.4 62.9 %copy-start.27 = (s32[512]{0:T(512)}, s32[512]{0:T(512)S(1)}, u32[]{:S(2)}) copy-start(s32[512]{0:T(512)S(1)} %get-tuple-element.233) | copy-start | bytes 6148
  29.4 64.7 %copy-start.25 = (s32[512]{0:T(512)}, s32[512]{0:T(512)S(1)}, u32[]{:S(2)}) copy-start(s32[512]{0:T(512)S(1)} %get-tuple-element.234) | copy-start | bytes 6148
  29.4 66.6 %copy-start.24 = (s32[512]{0:T(512)}, s32[512]{0:T(512)S(1)}, u32[]{:S(2)}) copy-start(s32[512]{0:T(512)S(1)} %get-tuple-element.229) | copy-start | bytes 6148
  37.4 7.9 %copy-start.21 = (f32[512]{0:T(512)}, f32[512]{0:T(512)S(1)}, u32[]{:S(2)}) copy-start(f32[512]{0:T(512)S(1)} %iota_add_fusion) | copy-start | bytes 6148
  37.7 7.6 %copy-start.9 = (f32[16,32]{0,1:T(8,128)}, f32[16,32]{0,1:T(8,128)S(1)}, u32[]{:S(2)}) copy-start(f32[16,32]{0,1:T(8,128)S(1)} %copy.98) | copy-start | bytes 6148
  64.1 39.2 %copy-start.40 = (pred[512]{0:T(512)(128)(4,1)S(1)}, pred[512]{0:T(512)(128)(4,1)}, u32[]{:S(2)}) copy-start(pred[512]{0:T(512)(128)(4,1)} %get-tuple-element.258) | copy-start | bytes 1540
  76.6 26.6 %collective-permute-start = (bf16[3,2,512]{2,1,0:T(2,128)(2,1)S(1)}, bf16[3,2,512]{2,1,0:T(2,128)(2,1)S(1)}, u32[]{:S(2)}, u32[]{:S(2)}) collective-permute-start(bf16[3,2,512]{2,1,0:T(2,128)(2,1)S(1)} %slice.154), channel_id=1, source_target_pairs={{0,16},{16,32},{32,48},{48,64},{64,80},{80,96},{96,112},{112,128},... | collective-permute-start | bytes 18440 | tf_op jit(solution)/shard_map/ppermute | solution.py:15
  110.8 43.4 %collective-permute-start.8 = (bf16[512,512]{1,0:T(8,128)(2,1)}, bf16[512,512]{1,0:T(8,128)(2,1)}, u32[]{:S(2)}, u32[]{:S(2)}) collective-permute-start(bf16[512,512]{1,0:T(8,128)(2,1)} %fusion.68), channel_id=1, source_target_pairs={{0,128},{16,144},{32,160},{48,176},{64,192},{80,208},{96,224},{112... | collective-permute-start | bytes 1572872 | tf_op jit(solution)/shard_map/ppermute | solution.py:15
  125.7 146.4 %collective-permute-start.7 = (bf16[512,512]{1,0:T(8,128)(2,1)}, bf16[512,512]{1,0:T(8,128)(2,1)}, u32[]{:S(2)}, u32[]{:S(2)}) collective-permute-start(bf16[512,512]{1,0:T(8,128)(2,1)} %fusion.68), channel_id=1, source_target_pairs={{0,112},{16,128},{32,144},{48,160},{64,176},{80,192},{96,208},{112... | collective-permute-start | bytes 1572872 | tf_op jit(solution)/shard_map/ppermute | solution.py:15
  129.7 219.2 %collective-permute-start.6 = (bf16[512,512]{1,0:T(8,128)(2,1)}, bf16[512,512]{1,0:T(8,128)(2,1)}, u32[]{:S(2)}, u32[]{:S(2)}) collective-permute-start(bf16[512,512]{1,0:T(8,128)(2,1)} %fusion.68), channel_id=1, source_target_pairs={{0,96},{16,112},{32,128},{48,144},{64,160},{80,176},{96,192},{112,... | collective-permute-start | bytes 1572872 | tf_op jit(solution)/shard_map/ppermute | solution.py:15
  132.8 226.8 %collective-permute-start.5 = (bf16[512,512]{1,0:T(8,128)(2,1)}, bf16[512,512]{1,0:T(8,128)(2,1)}, u32[]{:S(2)}, u32[]{:S(2)}) collective-permute-start(bf16[512,512]{1,0:T(8,128)(2,1)} %fusion.68), channel_id=1, source_target_pairs={{0,80},{16,96},{32,112},{48,128},{64,144},{80,160},{96,176},{112,1... | collective-permute-start | bytes 1572872 | tf_op jit(solution)/shard_map/ppermute | solution.py:15
  134.7 301.4 %collective-permute-start.4 = (bf16[512,512]{1,0:T(8,128)(2,1)}, bf16[512,512]{1,0:T(8,128)(2,1)}, u32[]{:S(2)}, u32[]{:S(2)}) collective-permute-start(bf16[512,512]{1,0:T(8,128)(2,1)} %fusion.68), channel_id=1, source_target_pairs={{0,64},{16,80},{32,96},{48,112},{64,128},{80,144},{96,160},{112,17... | collective-permute-start | bytes 1572872 | tf_op jit(solution)/shard_map/ppermute | solution.py:15
  141.3 4.0 copy-start.1
  141.3 4.9 copy-start.8
  144.1 4.7 copy-start.7
  148.7 2.5 copy-start.43
  148.7 2.9 copy-start.3
  148.8 3.0 copy-start.5
  148.8 3.0 copy-start.6
  151.2 199.5 %copy-start.41 = (f32[128]{0:T(128)S(1)}, f32[128]{0:T(128)}, u32[]{:S(2)}) copy-start(f32[128]{0:T(128)} %get-tuple-element.274) | copy-start | bytes 1540
  151.3 199.9 %copy-start.4 = (bf16[128,512]{0,1:T(8,128)(2,1)S(1)}, bf16[128,512]{0,1:T(8,128)(2,1)}, u32[]{:S(2)}) copy-start(bf16[128,512]{0,1:T(8,128)(2,1)} %copy.105) | copy-start | bytes 393220
  154.2 199.5 %copy-start.38 = (s32[512]{0:T(512)S(1)}, s32[512]{0:T(512)}, u32[]{:S(2)}) copy-start(s32[512]{0:T(512)} %copy-done.37) | copy-start | bytes 6148
  154.2 299.2 %collective-permute-start.3 = (bf16[512,512]{1,0:T(8,128)(2,1)}, bf16[512,512]{1,0:T(8,128)(2,1)}, u32[]{:S(2)}, u32[]{:S(2)}) collective-permute-start(bf16[512,512]{1,0:T(8,128)(2,1)} %fusion.68), channel_id=1, source_target_pairs={{0,48},{16,64},{32,80},{48,96},{64,112},{80,128},{96,144},{112,160... | collective-permute-start | bytes 1572872 | tf_op jit(solution)/shard_map/ppermute | solution.py:15
  272.0 202.8 %collective-permute-start.2 = (bf16[512,512]{1,0:T(8,128)(2,1)}, bf16[512,512]{1,0:T(8,128)(2,1)}, u32[]{:S(2)}, u32[]{:S(2)}) collective-permute-start(bf16[512,512]{1,0:T(8,128)(2,1)} %fusion.68), channel_id=1, source_target_pairs={{0,32},{16,48},{32,64},{48,80},{64,96},{80,112},{96,128},{112,144}... | collective-permute-start | bytes 1572872 | tf_op jit(solution)/shard_map/ppermute | solution.py:15
  348.9 137.0 %collective-permute-start.1 = (bf16[512,512]{1,0:T(8,128)(2,1)}, bf16[512,512]{1,0:T(8,128)(2,1)}, u32[]{:S(2)}, u32[]{:S(2)}) collective-permute-start(bf16[512,512]{1,0:T(8,128)(2,1)} %fusion.68), channel_id=1, source_target_pairs={{0,16},{16,32},{32,48},{48,64},{64,80},{80,96},{96,112},{112,128},... | collective-permute-start | bytes 1572872 | tf_op jit(solution)/shard_map/ppermute | solution.py:15
  353.7 3.3 copy-start.34
  357.0 2.6 copy-start.32
  359.6 76.5 %copy-start.30 = (s32[512]{0:T(512)S(1)}, s32[512]{0:T(512)}, u32[]{:S(2)}) copy-start(s32[512]{0:T(512)} %copy-done.29) | copy-start | bytes 6148
  362.3 91.0 %copy-start.28 = (s32[512]{0:T(512)S(1)}, s32[512]{0:T(512)}, u32[]{:S(2)}) copy-start(s32[512]{0:T(512)} %copy-done.27) | copy-start | bytes 6148
  438.8 36.0 %copy-start.26 = (s32[512]{0:T(512)S(1)}, s32[512]{0:T(512)}, u32[]{:S(2)}) copy-start(s32[512]{0:T(512)} %copy-done.25) | copy-start | bytes 6148
  477.5 12.4 %copy-start.10 = (f32[16,32]{0,1:T(8,128)S(1)}, f32[16,32]{0,1:T(8,128)}, u32[]{:S(2)}) copy-start(f32[16,32]{0,1:T(8,128)} %copy-done.9) | copy-start | bytes 6148
  477.5 12.4 %copy-start.13 = (f32[16,32]{0,1:T(8,128)S(1)}, f32[16,32]{0,1:T(8,128)}, u32[]{:S(2)}) copy-start(f32[16,32]{0,1:T(8,128)} %copy.121) | copy-start | bytes 6148
  477.5 12.4 %copy-start.14 = (f32[16,32]{0,1:T(8,128)S(1)}, f32[16,32]{0,1:T(8,128)}, u32[]{:S(2)}) copy-start(f32[16,32]{0,1:T(8,128)} %copy.119) | copy-start | bytes 6148
  477.5 12.4 %copy-start.15 = (f32[16,32]{0,1:T(8,128)S(1)}, f32[16,32]{0,1:T(8,128)}, u32[]{:S(2)}) copy-start(f32[16,32]{0,1:T(8,128)} %copy.117) | copy-start | bytes 6148
  477.5 12.4 %copy-start.16 = (f32[16,32]{0,1:T(8,128)S(1)}, f32[16,32]{0,1:T(8,128)}, u32[]{:S(2)}) copy-start(f32[16,32]{0,1:T(8,128)} %copy.115) | copy-start | bytes 6148
  477.5 12.4 %copy-start.17 = (f32[16,32]{0,1:T(8,128)S(1)}, f32[16,32]{0,1:T(8,128)}, u32[]{:S(2)}) copy-start(f32[16,32]{0,1:T(8,128)} %copy.113) | copy-start | bytes 6148
  477.5 12.4 %copy-start.18 = (f32[16,32]{0,1:T(8,128)S(1)}, f32[16,32]{0,1:T(8,128)}, u32[]{:S(2)}) copy-start(f32[16,32]{0,1:T(8,128)} %copy.111) | copy-start | bytes 6148
  477.5 12.4 %copy-start.19 = (f32[16,32]{0,1:T(8,128)S(1)}, f32[16,32]{0,1:T(8,128)}, u32[]{:S(2)}) copy-start(f32[16,32]{0,1:T(8,128)} %copy.109) | copy-start | bytes 6148
  (6 other events, 9.3 us)
where the time goes:
time: 514 us; the launch traced here: 511 us
  waiting for transfers between devices  286 us (56%)
  local copies, waits for them, and re-layouts  81.7 us (16%)
  starting transfers between devices  67.4 us (13%)
  matrix products  29.4 us (6%)
  other arithmetic  16.7 us (3%)
  blocking collectives  14.7 us (3%)
  between operations  14.6 us (3%)
    ppermute x9, waiting for transfers between devices, shifted_2(): return lax.ppermute(block, axis, route)  280 us
    ppermute x9, starting transfers between devices, shifted_2(): return lax.ppermute(block, axis, route)  62 us
    unnamed x94, local copies, waits for them, and re-layouts  38.6 us
    dot_general x20, matrix products, contract(): jnp.einsum(pattern, left_side, right_side, precision=lax.Precision.HIGHEST)  29.4 us
    all_to_all x1, blocking collectives, local(): lax.all_to_all(payload, 'fsdp', split_axis=0, concat_axis=1, tiled=True)  14.7 us
    all_to_all x1, local copies, waits for them, and re-layouts, local(): lax.all_to_all(streams, 'fsdp', split_axis=2, concat_axis=1, tiled=True)  11.8 us
  transfers between devices with their start and end apart: 10, of which 7 were waited for; matrix products, arithmetic and copies ran while one was open for 12% of the time, Pallas kernels for 0%

commit v1 on v0

--- a/solution.py
+++ b/solution.py
@@ -7,6 +7,12 @@
 MODES = 16
 SHORT = 3
 SPAN = 8
+
+
+def swap_blocks(x, name, split, join):
+    shards = jnp.split(x, lax.axis_size(name), axis=split)
+    got = lax.all_to_all(jnp.stack(shards), name, 0, 0)
+    return jnp.concatenate(got, axis=join)
 
 
 def shifted_2(block, axis, distance):
@@ -80,7 +86,7 @@
     padded_marks = jnp.concatenate([jnp.full((margin,), -1, jnp.int32), segments])
     tile_start = tile_index * tile_rows
     tile_marks = lax.dynamic_slice_in_dim(segments, tile_start, tile_rows)
-    local_streams = lax.all_to_all(streams, "fsdp", split_axis=2, concat_axis=1, tiled=True)
+    local_streams = swap_blocks(streams, "fsdp", 2, 1)
     before_rows = shifted_2(local_streams[:, tile_rows - margin :, :], "ctx", 1)
     before_marks = lax.dynamic_slice_in_dim(padded_marks, tile_start, margin)
     queries, gated_prod = featurize(

time: 514 us -> 489 us (0.951)
  waiting for transfers between devices: 286 us -> 207 us
  starting transfers between devices: 67.4 us -> 139 us
  local copies, waits for them, and re-layouts: 81.7 us -> 58.4 us
  blocking collectives: 14.7 us -> 20.1 us
    ppermute x9, waiting for transfers between devices: 280 us -> 201 us  [shifted_2(): return lax.ppermute(block, axis, route)]
    ppermute x9, starting transfers between devices: 62 us -> 134 us  [shifted_2(): return lax.ppermute(block, axis, route)]
    unnamed x94 -> x108, local copies, waits for them, and re-layouts: 38.6 us -> 25.8 us
    all_to_all x1, local copies, waits for them, and re-layouts: 11.8 us -> 1.51 us  [swap_blocks(): got = lax.all_to_all(jnp.stack(shards), name, 0, 0)]
    all_to_all x1, blocking collectives: 14.7 us -> 20.1 us  [local(): lax.all_to_all(payload, 'fsdp', split_axis=0, concat_axis=1, tiled=True)]
    another operation x8 -> x9, local copies, waits for them, and re-layouts: 8.79 us -> 10.4 us
  transfers between devices with their start and end apart: 10 -> 10, of which waited for: 7 -> 8; matrix products, arithmetic and copies ran while one was open for 12% -> 12% of each run, Pallas kernels for 0% -> 0%
where the time goes in v1:
time: 489 us; the launch traced here: 487 us
  waiting for transfers between devices  207 us (42%)
  starting transfers between devices  139 us (28%)
  local copies, waits for them, and re-layouts  58.4 us (12%)
  matrix products  28.8 us (6%)
  blocking collectives  20.1 us (4%)
  other arithmetic  17.2 us (4%)
  between operations  15.4 us (3%)
    ppermute x9, waiting for transfers between devices, shifted_2(): return lax.ppermute(block, axis, route)  201 us
    ppermute x9, starting transfers between devices, shifted_2(): return lax.ppermute(block, axis, route)  134 us
    dot_general x20, matrix products, contract(): jnp.einsum(pattern, left_side, right_side, precision=lax.Precision.HIGHEST)  28.8 us
    unnamed x108, local copies, waits for them, and re-layouts  25.8 us
    all_to_all x1, blocking collectives, local(): lax.all_to_all(payload, 'fsdp', split_axis=0, concat_axis=1, tiled=True)  20.1 us
  transfers between devices with their start and end apart: 10, of which 8 were waited for; matrix products, arithmetic and copies ran while one was open for 12% of the time, Pallas kernels for 0%

profile of v1, /device:TPU:4, one launch (start us, length us, event | category | flops | bytes accessed | tf_op | source)
XLA Modules:
  0.0 486.9 jit_solution(18244165462619225754)
XLA Ops:
  0.0 1.5 bitcast_dynamic-update-slice_fusion.15
  1.5 1.5 bitcast_dynamic-update-slice_fusion.14
  3.1 1.5 bitcast_dynamic-update-slice_fusion.13
  4.6 1.5 bitcast_dynamic-update-slice_fusion.12
  6.2 1.5 bitcast_dynamic-update-slice_fusion.11
  7.7 1.6 bitcast_dynamic-update-slice_fusion.10
  9.3 1.5 bitcast_dynamic-update-slice_fusion.9
  10.8 1.5 bitcast_dynamic-update-slice_fusion.8
  12.3 1.5 bitcast_dynamic-update-slice_fusion.7
  13.9 1.5 bitcast_dynamic-update-slice_fusion.6
  16.9 1.5 bitcast_dynamic-update-slice_fusion.4
  18.5 1.5 bitcast_dynamic-update-slice_fusion.3
  24.6 5.4 %all-to-all-start = ((bf16[16,3,32,512]{3,2,1,0:T(8,128)(2,1)}), bf16[16,3,32,512]{3,2,1,0:T(8,128)(2,1)}, u32[]{:S(2)}, u32[]{:S(2)}) async-start(bf16[16,3,32,512]{3,2,1,0:T(8,128)(2,1)} %bitcast_dynamic-update-slice_fusion), calls=%async_computation | async-start | bytes 3145728 | tf_op jit(solution)/shard_map/all_to_all | solution.py:14
  34.1 2.5 compare_convert_fusion.18
  42.5 3.7 fusion.87
  46.2 6.1 %all-to-all-done = bf16[16,3,32,512]{3,2,1,0:T(8,128)(2,1)} async-done(((bf16[16,3,32,512]{3,2,1,0:T(8,128)(2,1)}), bf16[16,3,32,512]{3,2,1,0:T(8,128)(2,1)}, u32[]{:S(2)}, u32[]{:S(2)}) %all-to-all-start) | async-done | bytes 1572896 | tf_op jit(solution)/shard_map/all_to_all | solution.py:14
  55.0 3.8 collective-permute-start
  82.2 3.8 multiply_add_fusion
  87.8 1.8 fusion.125
  89.6 7.7 %collective-permute-start.3 = (bf16[512,512]{1,0:T(8,128)(2,1)}, bf16[512,512]{1,0:T(8,128)(2,1)}, u32[]{:S(2)}, u32[]{:S(2)}) collective-permute-start(bf16[512,512]{1,0:T(8,128)(2,1)} %fusion.68), channel_id=1, source_target_pairs={{0,48},{16,64},{32,80},{48,96},{64,112},{80,128},{96,144},{112,160... | collective-permute-start | bytes 1572872 | tf_op jit(solution)/shard_map/ppermute | solution.py:21
  97.4 9.1 %collective-permute-start.4 = (bf16[512,512]{1,0:T(8,128)(2,1)}, bf16[512,512]{1,0:T(8,128)(2,1)}, u32[]{:S(2)}, u32[]{:S(2)}) collective-permute-start(bf16[512,512]{1,0:T(8,128)(2,1)} %fusion.68), channel_id=1, source_target_pairs={{0,64},{16,80},{32,96},{48,112},{64,128},{80,144},{96,160},{112,17... | collective-permute-start | bytes 1572872 | tf_op jit(solution)/shard_map/ppermute | solution.py:21
  106.5 4.7 collective-permute-start.5
  111.2 2.8 collective-permute-start.6
  114.1 2.1 collective-permute-start.7
  118.1 1.7 copy.102
  124.1 2.5 fusion.40
  126.6 2.5 fusion.46
  129.6 2.5 fusion.34
  132.1 8.3 %collective-permute-done.3 = bf16[512,512]{1,0:T(8,128)(2,1)} collective-permute-done((bf16[512,512]{1,0:T(8,128)(2,1)}, bf16[512,512]{1,0:T(8,128)(2,1)}, u32[]{:S(2)}, u32[]{:S(2)}) %collective-permute-start.3) | collective-permute-done | bytes 524320 | tf_op jit(solution)/shard_map/ppermute | solution.py:21
  140.4 5.6 %collective-permute-start.8 = (bf16[512,512]{1,0:T(8,128)(2,1)}, bf16[512,512]{1,0:T(8,128)(2,1)}, u32[]{:S(2)}, u32[]{:S(2)}) collective-permute-start(bf16[512,512]{1,0:T(8,128)(2,1)} %fusion.68), channel_id=1, source_target_pairs={{0,128},{16,144},{32,160},{48,176},{64,192},{80,208},{96,224},{112... | collective-permute-start | bytes 1572872 | tf_op jit(solution)/shard_map/ppermute | solution.py:21
  146.0 18.1 %collective-permute-done.4 = bf16[512,512]{1,0:T(8,128)(2,1)} collective-permute-done((bf16[512,512]{1,0:T(8,128)(2,1)}, bf16[512,512]{1,0:T(8,128)(2,1)}, u32[]{:S(2)}, u32[]{:S(2)}) %collective-permute-start.4) | collective-permute-done | bytes 524320 | tf_op jit(solution)/shard_map/ppermute | solution.py:21
  164.1 26.6 %collective-permute-start.1 = (bf16[512,512]{1,0:T(8,128)(2,1)}, bf16[512,512]{1,0:T(8,128)(2,1)}, u32[]{:S(2)}, u32[]{:S(2)}) collective-permute-start(bf16[512,512]{1,0:T(8,128)(2,1)} %fusion.68), channel_id=1, source_target_pairs={{0,16},{16,32},{32,48},{48,64},{64,80},{80,96},{96,112},{112,128},... | collective-permute-start | bytes 1572872 | tf_op jit(solution)/shard_map/ppermute | solution.py:21
  190.7 48.6 %collective-permute-done.5 = bf16[512,512]{1,0:T(8,128)(2,1)} collective-permute-done((bf16[512,512]{1,0:T(8,128)(2,1)}, bf16[512,512]{1,0:T(8,128)(2,1)}, u32[]{:S(2)}, u32[]{:S(2)}) %collective-permute-start.5) | collective-permute-done | bytes 524320 | tf_op jit(solution)/shard_map/ppermute | solution.py:21
  239.3 71.5 %collective-permute-start.2 = (bf16[512,512]{1,0:T(8,128)(2,1)}, bf16[512,512]{1,0:T(8,128)(2,1)}, u32[]{:S(2)}, u32[]{:S(2)}) collective-permute-start(bf16[512,512]{1,0:T(8,128)(2,1)} %fusion.68), channel_id=1, source_target_pairs={{0,32},{16,48},{32,64},{48,80},{64,96},{80,112},{96,128},{112,144}... | collective-permute-start | bytes 1572872 | tf_op jit(solution)/shard_map/ppermute | solution.py:21
  311.2 2.5 fusion.52
  313.7 2.6 conditional.10
  316.4 2.7 conditional.11
  319.1 2.7 conditional.12
  321.8 2.7 conditional.13
  324.6 81.7 %collective-permute-done.7 = bf16[512,512]{1,0:T(8,128)(2,1)} collective-permute-done((bf16[512,512]{1,0:T(8,128)(2,1)}, bf16[512,512]{1,0:T(8,128)(2,1)}, u32[]{:S(2)}, u32[]{:S(2)}) %collective-permute-start.7) | collective-permute-done | bytes 524320 | tf_op jit(solution)/shard_map/ppermute | solution.py:21
  406.3 2.7 conditional.14
  409.0 4.5 collective-permute-done.8
  413.5 25.6 %collective-permute-done.1 = bf16[512,512]{1,0:T(8,128)(2,1)} collective-permute-done((bf16[512,512]{1,0:T(8,128)(2,1)}, bf16[512,512]{1,0:T(8,128)(2,1)}, u32[]{:S(2)}, u32[]{:S(2)}) %collective-permute-start.1) | collective-permute-done | bytes 524320 | tf_op jit(solution)/shard_map/ppermute | solution.py:21
  439.1 2.6 conditional.8
  441.7 14.6 %collective-permute-done.2 = bf16[512,512]{1,0:T(8,128)(2,1)} collective-permute-done((bf16[512,512]{1,0:T(8,128)(2,1)}, bf16[512,512]{1,0:T(8,128)(2,1)}, u32[]{:S(2)}, u32[]{:S(2)}) %collective-permute-start.2) | collective-permute-done | bytes 524320 | tf_op jit(solution)/shard_map/ppermute | solution.py:21
  456.4 4.2 conditional.9
  460.6 3.3 fusion.30
  466.0 20.1 %all_to_all.24 = bf16[16,32,512]{2,1,0:T(8,128)(2,1)S(1)} all-to-all(bf16[16,32,512]{2,1,0:T(8,128)(2,1)S(1)} %bitcast.150), channel_id=1, replica_groups=mesh['ctx'=32,'fsdp'=16] {'fsdp'}, dimensions={0} | all-to-all | bytes 1048576 | tf_op jit(solution)/shard_map/all_to_all | solution.py:137
  (179 shorter events, 59.3 us)
Async XLA Ops:
  24.6 5.5 %copy-start.12 = (s32[16384]{0:T(1024)S(1)}, s32[16384]{0:T(1024)}, u32[]{:S(2)}) copy-start(s32[16384]{0:T(1024)} %param.23) | copy-start | bytes 196612
  24.6 13.0 %copy-start.23 = (f32[3,3,512]{2,1,0:T(4,128)S(1)}, f32[3,3,512]{2,1,0:T(4,128)}, u32[]{:S(2)}) copy-start(f32[3,3,512]{2,1,0:T(4,128)} %param.24) | copy-start | bytes 55300
  24.6 13.6 %copy-start.13 = (f32[32,16]{0,1:T(8,128)S(1)}, f32[32,16]{0,1:T(8,128)}, u32[]{:S(2)}) copy-start(f32[32,16]{0,1:T(8,128)} %param.25) | copy-start | bytes 6148
  24.6 13.6 %copy-start.24 = (f32[32,16]{0,1:T(8,128)S(1)}, f32[32,16]{0,1:T(8,128)}, u32[]{:S(2)}) copy-start(f32[32,16]{0,1:T(8,128)} %param.26) | copy-start | bytes 6148
  24.6 27.7 %all-to-all-start = ((bf16[16,3,32,512]{3,2,1,0:T(8,128)(2,1)}), bf16[16,3,32,512]{3,2,1,0:T(8,128)(2,1)}, u32[]{:S(2)}, u32[]{:S(2)}) async-start(bf16[16,3,32,512]{3,2,1,0:T(8,128)(2,1)} %bitcast_dynamic-update-slice_fusion), calls=%async_computation | async-start | bytes 3145728 | tf_op jit(solution)/shard_map/all_to_all | solution.py:14
  30.2 31.1 %copy-start.38 = (s32[512]{0:T(512)}, s32[512]{0:T(512)S(1)}, u32[]{:S(2)}) copy-start(s32[512]{0:T(512)S(1)} %get-tuple-element.233) | copy-start | bytes 6148
  30.2 33.1 %copy-start.36 = (s32[512]{0:T(512)}, s32[512]{0:T(512)S(1)}, u32[]{:S(2)}) copy-start(s32[512]{0:T(512)S(1)} %get-tuple-element.232) | copy-start | bytes 6148
  30.2 35.0 %copy-start.34 = (s32[512]{0:T(512)}, s32[512]{0:T(512)S(1)}, u32[]{:S(2)}) copy-start(s32[512]{0:T(512)S(1)} %get-tuple-element.231) | copy-start | bytes 6148
  30.2 36.9 %copy-start.32 = (s32[512]{0:T(512)}, s32[512]{0:T(512)S(1)}, u32[]{:S(2)}) copy-start(s32[512]{0:T(512)S(1)} %get-tuple-element.230) | copy-start | bytes 6148
  30.2 38.8 %copy-start.30 = (s32[512]{0:T(512)}, s32[512]{0:T(512)S(1)}, u32[]{:S(2)}) copy-start(s32[512]{0:T(512)S(1)} %get-tuple-element.237) | copy-start | bytes 6148
  30.2 40.8 %copy-start.28 = (s32[512]{0:T(512)}, s32[512]{0:T(512)S(1)}, u32[]{:S(2)}) copy-start(s32[512]{0:T(512)S(1)} %get-tuple-element.236) | copy-start | bytes 6148
  30.2 42.7 %copy-start.26 = (s32[512]{0:T(512)}, s32[512]{0:T(512)S(1)}, u32[]{:S(2)}) copy-start(s32[512]{0:T(512)S(1)} %get-tuple-element.229) | copy-start | bytes 6148
  30.2 44.6 %copy-start.25 = (s32[512]{0:T(512)}, s32[512]{0:T(512)S(1)}, u32[]{:S(2)}) copy-start(s32[512]{0:T(512)S(1)} %get-tuple-element.234) | copy-start | bytes 6148
  36.7 5.8 %copy-start.22 = (f32[512]{0:T(512)}, f32[512]{0:T(512)S(1)}, u32[]{:S(2)}) copy-start(f32[512]{0:T(512)S(1)} %iota_add_fusion) | copy-start | bytes 6148
  55.0 27.2 %collective-permute-start = (bf16[3,2,512]{2,1,0:T(2,128)(2,1)S(1)}, bf16[3,2,512]{2,1,0:T(2,128)(2,1)S(1)}, u32[]{:S(2)}, u32[]{:S(2)}) collective-permute-start(bf16[3,2,512]{2,1,0:T(2,128)(2,1)S(1)} %slice.154), channel_id=1, source_target_pairs={{0,16},{16,32},{32,48},{48,64},{64,80},{80,96},{96,112},{112,128},... | collective-permute-start | bytes 18440 | tf_op jit(solution)/shard_map/ppermute | solution.py:21
  89.6 50.7 %collective-permute-start.3 = (bf16[512,512]{1,0:T(8,128)(2,1)}, bf16[512,512]{1,0:T(8,128)(2,1)}, u32[]{:S(2)}, u32[]{:S(2)}) collective-permute-start(bf16[512,512]{1,0:T(8,128)(2,1)} %fusion.68), channel_id=1, source_target_pairs={{0,48},{16,64},{32,80},{48,96},{64,112},{80,128},{96,144},{112,160... | collective-permute-start | bytes 1572872 | tf_op jit(solution)/shard_map/ppermute | solution.py:21
  97.4 66.7 %collective-permute-start.4 = (bf16[512,512]{1,0:T(8,128)(2,1)}, bf16[512,512]{1,0:T(8,128)(2,1)}, u32[]{:S(2)}, u32[]{:S(2)}) collective-permute-start(bf16[512,512]{1,0:T(8,128)(2,1)} %fusion.68), channel_id=1, source_target_pairs={{0,64},{16,80},{32,96},{48,112},{64,128},{80,144},{96,160},{112,17... | collective-permute-start | bytes 1572872 | tf_op jit(solution)/shard_map/ppermute | solution.py:21
  106.5 132.8 %collective-permute-start.5 = (bf16[512,512]{1,0:T(8,128)(2,1)}, bf16[512,512]{1,0:T(8,128)(2,1)}, u32[]{:S(2)}, u32[]{:S(2)}) collective-permute-start(bf16[512,512]{1,0:T(8,128)(2,1)} %fusion.68), channel_id=1, source_target_pairs={{0,80},{16,96},{32,112},{48,128},{64,144},{80,160},{96,176},{112,1... | collective-permute-start | bytes 1572872 | tf_op jit(solution)/shard_map/ppermute | solution.py:21
  111.2 210.6 %collective-permute-start.6 = (bf16[512,512]{1,0:T(8,128)(2,1)}, bf16[512,512]{1,0:T(8,128)(2,1)}, u32[]{:S(2)}, u32[]{:S(2)}) collective-permute-start(bf16[512,512]{1,0:T(8,128)(2,1)} %fusion.68), channel_id=1, source_target_pairs={{0,96},{16,112},{32,128},{48,144},{64,160},{80,176},{96,192},{112,... | collective-permute-start | bytes 1572872 | tf_op jit(solution)/shard_map/ppermute | solution.py:21
  114.1 292.2 %collective-permute-start.7 = (bf16[512,512]{1,0:T(8,128)(2,1)}, bf16[512,512]{1,0:T(8,128)(2,1)}, u32[]{:S(2)}, u32[]{:S(2)}) collective-permute-start(bf16[512,512]{1,0:T(8,128)(2,1)} %fusion.68), channel_id=1, source_target_pairs={{0,112},{16,128},{32,144},{48,160},{64,176},{80,192},{96,208},{112... | collective-permute-start | bytes 1572872 | tf_op jit(solution)/shard_map/ppermute | solution.py:21
  119.8 3.9 copy-start.2
  119.8 3.9 copy-start.43
  119.8 4.3 copy-start.8
  126.6 2.5 copy-start.21
  126.6 2.5 copy-start.42
  126.6 2.5 copy-start.44
  126.6 2.9 copy-start.4
  126.6 2.9 copy-start.6
  126.6 2.9 copy-start.7
  129.5 181.3 %copy-start.41 = (f32[128]{0:T(128)S(1)}, f32[128]{0:T(128)}, u32[]{:S(2)}) copy-start(f32[128]{0:T(128)} %get-tuple-element.274) | copy-start | bytes 1540
  129.6 181.7 %copy-start.5 = (bf16[128,512]{0,1:T(8,128)(2,1)S(1)}, bf16[128,512]{0,1:T(8,128)(2,1)}, u32[]{:S(2)}) copy-start(bf16[128,512]{0,1:T(8,128)(2,1)} %copy.102) | copy-start | bytes 393220
  140.4 273.1 %collective-permute-start.8 = (bf16[512,512]{1,0:T(8,128)(2,1)}, bf16[512,512]{1,0:T(8,128)(2,1)}, u32[]{:S(2)}, u32[]{:S(2)}) collective-permute-start(bf16[512,512]{1,0:T(8,128)(2,1)} %fusion.68), channel_id=1, source_target_pairs={{0,128},{16,144},{32,160},{48,176},{64,192},{80,208},{96,224},{112... | collective-permute-start | bytes 1572872 | tf_op jit(solution)/shard_map/ppermute | solution.py:21
  164.1 275.0 %collective-permute-start.1 = (bf16[512,512]{1,0:T(8,128)(2,1)}, bf16[512,512]{1,0:T(8,128)(2,1)}, u32[]{:S(2)}, u32[]{:S(2)}) collective-permute-start(bf16[512,512]{1,0:T(8,128)(2,1)} %fusion.68), channel_id=1, source_target_pairs={{0,16},{16,32},{32,48},{48,64},{64,80},{80,96},{96,112},{112,128},... | collective-permute-start | bytes 1572872 | tf_op jit(solution)/shard_map/ppermute | solution.py:21
  239.3 217.0 %collective-permute-start.2 = (bf16[512,512]{1,0:T(8,128)(2,1)}, bf16[512,512]{1,0:T(8,128)(2,1)}, u32[]{:S(2)}, u32[]{:S(2)}) collective-permute-start(bf16[512,512]{1,0:T(8,128)(2,1)} %fusion.68), channel_id=1, source_target_pairs={{0,32},{16,48},{32,64},{48,80},{64,96},{80,112},{96,128},{112,144}... | collective-permute-start | bytes 1572872 | tf_op jit(solution)/shard_map/ppermute | solution.py:21
  313.7 2.7 copy-start.37
  316.4 2.7 copy-start.35
  319.1 2.7 copy-start.33
  321.8 84.5 %copy-start.31 = (s32[512]{0:T(512)S(1)}, s32[512]{0:T(512)}, u32[]{:S(2)}) copy-start(s32[512]{0:T(512)} %copy-done.30) | copy-start | bytes 6148
  406.3 7.2 %copy-start.29 = (s32[512]{0:T(512)S(1)}, s32[512]{0:T(512)}, u32[]{:S(2)}) copy-start(s32[512]{0:T(512)} %copy-done.28) | copy-start | bytes 6148
  413.5 25.6 %copy-start.27 = (s32[512]{0:T(512)S(1)}, s32[512]{0:T(512)}, u32[]{:S(2)}) copy-start(s32[512]{0:T(512)} %copy-done.26) | copy-start | bytes 6148
  456.3 4.2 copy-start.11
  456.3 4.2 copy-start.14
  456.3 4.2 copy-start.15
  456.3 4.2 copy-start.16
  456.3 4.3 copy-start.17
  456.4 4.3 copy-start.18
  456.4 4.3 copy-start.19
  456.4 4.3 copy-start.20
  (7 other events, 11.0 us)
